TPU v7x, 32 devices: a whole 2x2x4 slice. The times are simulated.
32 devices in a mesh: fsdp: 16 (over z, y, x), mp: 2 (over core).
Axes of the slice: x: 2, y: 2, z: 4, core: 2. Of those that a mesh axis runs over, the one named last changes fastest.
Arguments:
- values: bfloat16 [4096, 32], P('fsdp'), may hold values from -6 to 6
- lengths: int32 [64], P('fsdp'), may hold values from 1 to 64, 2560 in all
- w_in1: bfloat16 [64, 1280], P(None, 'fsdp'), may hold values from -0.75 to 0.75
- b_in1: bfloat16 [1280], P('fsdp'), may hold values from -3 to 3
- w_in2: bfloat16 [1280, 1280], P('fsdp'), may hold values from -0.15625 to 0.15625
- b_in2: bfloat16 [1280], P('fsdp'), may hold values from -3 to 3
- w_res: bfloat16 [64, 1280], P(None, 'fsdp'), may hold values from -0.75 to 0.75
- g_attn: bfloat16 [1280], P('fsdp'), may hold values from 0.099609375 to 1.8984375
- w_qkv: bfloat16 [1280, 3, 1280], P('fsdp', None, 'mp'), may hold values from -0.15625 to 0.15625
- w_out: bfloat16 [1280, 1280], P('mp', 'fsdp'), may hold values from -0.5 to 0.5
- g_mlp: bfloat16 [1280], P('fsdp'), may hold values from 0.099609375 to 1.8984375
- w_up: bfloat16 [1280, 1280], P('fsdp', 'mp'), may hold values from -0.15625 to 0.15625
- w_down: bfloat16 [1280, 1280], P('mp', 'fsdp'), may hold values from -0.25 to 0.25
- cotangent: bfloat16 [4096, 1280], P('fsdp'), may hold values from -6 to 6
Outputs:
- output: bfloat16 [4096, 1280], P('fsdp')
- d_values: float32 [4096, 32], P('fsdp')
- d_w_in1: float32 [64, 1280], P(None, 'fsdp')
- d_b_in1: float32 [1280], P('fsdp')
- d_w_in2: float32 [1280, 1280], P('fsdp')
- d_b_in2: float32 [1280], P('fsdp')
- d_w_res: float32 [64, 1280], P(None, 'fsdp')
- d_g_attn: float32 [1280], P('fsdp')
- d_w_qkv: float32 [1280, 3, 1280], P('fsdp', None, 'mp')
- d_w_out: float32 [1280, 1280], P('mp', 'fsdp')
- d_g_mlp: float32 [1280], P('fsdp')
- d_w_up: float32 [1280, 1280], P('fsdp', 'mp')
- d_w_down: float32 [1280, 1280], P('mp', 'fsdp')
Inputs may be any that keep to these rules, and one draw needn't show every extreme that they name: `lengths`: patches of series s; its padded slots come first.
All inputs are finite; a program needn't handle non-finite values. No bound on the sum of `lengths` on one device may be relied on, other than what follows from the above.
Results may differ from a plain program's by a relative error of at most 0.014.
Values may be sent and summed in bfloat16 or wider, within the bound.
A program may use at most 192 MiB of HBM per device.

v0:
```python
import jax
import jax.numpy as jnp
from jax import lax
from jax.sharding import PartitionSpec as P

HD = 80


def rotate(vectors, places):
    half_width = vectors.shape[-1] // 2
    frequency = 10000.0 ** (-2.0 * jnp.arange(half_width, dtype=jnp.float32) / vectors.shape[-1])
    angles = places[:, :, None, None] * frequency
    cosine = jnp.cos(angles)
    sine_val = jnp.sin(angles)
    first_half = vectors[..., :half_width]
    second_half = vectors[..., half_width:]
    return jnp.concatenate(
        [
            first_half * cosine - second_half * sine_val,
            second_half * cosine + first_half * sine_val,
        ],
        -1,
    )


def rms_norm(resid_rows, gain_vec):
    return (
        resid_rows
        * lax.rsqrt(jnp.mean(resid_rows * resid_rows, -1, keepdims=True) + 1e-06)
        * gain_vec
    )


def activate(up_rows):
    return jax.nn.gelu(up_rows, approximate=False)


def on_device(
    values,
    lengths,
    w_in1,
    b_in1,
    w_in2,
    b_in2,
    w_res,
    g_attn,
    w_qkv,
    w_out,
    g_mlp,
    w_up,
    w_down,
    cotangent,
):
    f32 = jnp.float32
    bf16 = jnp.bfloat16
    gathered = (
        lax.all_gather(w_in1, "fsdp", axis=1, tiled=True),
        lax.all_gather(b_in1, "fsdp", axis=0, tiled=True),
        lax.all_gather(w_in2, "fsdp", axis=0, tiled=True),
        lax.all_gather(b_in2, "fsdp", axis=0, tiled=True),
        lax.all_gather(w_res, "fsdp", axis=1, tiled=True),
        lax.all_gather(g_attn, "fsdp", axis=0, tiled=True),
        lax.all_gather(w_qkv, "fsdp", axis=0, tiled=True),
        lax.all_gather(w_out, "fsdp", axis=1, tiled=True),
        lax.all_gather(g_mlp, "fsdp", axis=0, tiled=True),
        lax.all_gather(w_up, "fsdp", axis=0, tiled=True),
        lax.all_gather(w_down, "fsdp", axis=1, tiled=True),
    )
    (
        full_in1,
        full_b1,
        full_in2,
        full_b2,
        full_res,
        full_gattn,
        full_qkv,
        full_out,
        full_gmlp,
        full_up,
        full_down,
    ) = gathered
    series = lengths.shape[0]
    seq_len = values.shape[0] // series
    patch_len = values.shape[1]
    slot_ids = jnp.arange(seq_len, dtype=jnp.int32)
    pad_count = seq_len - lengths
    padded = slot_ids[None, :] < pad_count[:, None]
    places = (slot_ids[None, :] - pad_count[:, None]).astype(f32)
    keep_mask = (1.0 - padded.astype(f32)).reshape(-1, 1)
    inputs = jnp.concatenate(
        [values.astype(f32) * keep_mask, jnp.broadcast_to(1.0 - keep_mask, values.shape)], 1
    ).astype(bf16)
    pre_act = jnp.dot(inputs, full_in1, preferred_element_type=f32) + full_b1.astype(f32)
    hidden = jax.nn.silu(pre_act).astype(bf16)
    resid0 = (
        jnp.dot(hidden, full_in2, preferred_element_type=f32)
        + full_b2.astype(f32)
        + jnp.dot(inputs, full_res, preferred_element_type=f32)
    )
    gain_attn = full_gattn.astype(f32)
    normed = rms_norm(resid0, gain_attn).astype(bf16)
    projected = jnp.einsum("td,dch->tch", normed, full_qkv, preferred_element_type=f32)
    local_heads = projected.shape[2] // HD
    head_shape = (series, seq_len, local_heads, HD)
    queries = rotate(projected[:, 0].reshape(head_shape), places).astype(bf16)
    key_rows = rotate(projected[:, 1].reshape(head_shape), places).astype(bf16)
    value_heads = projected[:, 2].reshape(head_shape).astype(bf16)
    causal = slot_ids[None, :] <= slot_ids[:, None]
    diagonal = slot_ids[None, :] == slot_ids[:, None]
    allowed = (causal[None] & (jnp.logical_not(padded)[:, None, :] | diagonal[None]))[:, None]
    scale = HD ** (-0.5)

    def score_block():
        raw = jnp.einsum("sqhe,skhe->shqk", queries, key_rows, preferred_element_type=f32) * scale
        return jnp.where(allowed, raw, -1e30)

    scores = score_block()
    row_max = jnp.max(scores, -1, keepdims=True)
    exponent = jnp.exp(scores - row_max)
    row_total = jnp.sum(exponent, -1, keepdims=True)
    log_total = row_max + jnp.log(row_total)
    attn_probs = (exponent / row_total).astype(bf16)
    attended = (
        jnp.einsum("shqk,skhe->sqhe", attn_probs, value_heads, preferred_element_type=f32)
        .reshape(-1, local_heads * HD)
        .astype(bf16)
    )
    branch_one = lax.psum(jnp.dot(attended, full_out, preferred_element_type=f32), "mp")
    resid1 = resid0 + branch_one
    gain_mlp = full_gmlp.astype(f32)
    normed2 = rms_norm(resid1, gain_mlp).astype(bf16)
    up_rows = jnp.dot(normed2, full_up, preferred_element_type=f32)
    mlp_hidden = activate(up_rows).astype(bf16)
    branch_two = lax.psum(
        jnp.dot(mlp_hidden, full_down, preferred_element_type=f32).astype(jnp.bfloat16), "mp"
    ).astype(jnp.float32)
    result = (resid1 + branch_two).astype(bf16)
    again = (
        lax.all_gather(w_in1, "fsdp", axis=1, tiled=True),
        lax.all_gather(b_in1, "fsdp", axis=0, tiled=True),
        lax.all_gather(w_in2, "fsdp", axis=0, tiled=True),
        lax.all_gather(b_in2, "fsdp", axis=0, tiled=True),
        lax.all_gather(w_res, "fsdp", axis=1, tiled=True),
        lax.all_gather(g_attn, "fsdp", axis=0, tiled=True),
        lax.all_gather(w_qkv, "fsdp", axis=0, tiled=True),
        lax.all_gather(w_out, "fsdp", axis=1, tiled=True),
        lax.all_gather(g_mlp, "fsdp", axis=0, tiled=True),
        lax.all_gather(w_up, "fsdp", axis=0, tiled=True),
        lax.all_gather(w_down, "fsdp", axis=1, tiled=True),
    )
    (
        back_in1,
        back_b1,
        back_in2,
        back_b2,
        back_res,
        back_gattn,
        back_qkv,
        back_out,
        back_gmlp,
        back_up,
        back_down,
    ) = again
    cot_rows = cotangent.astype(f32)
    grad_down = jnp.einsum("tf,td->fd", mlp_hidden, cotangent, preferred_element_type=f32)
    grad_hidden = jnp.einsum("td,fd->tf", cotangent, back_down, preferred_element_type=f32)
    unused_one, pull_mlp = jax.vjp(activate, up_rows)
    grad_up_rows = pull_mlp(grad_hidden)[0].astype(bf16)
    grad_up = jnp.einsum("td,tf->df", normed2, grad_up_rows, preferred_element_type=f32)
    norm_part2 = jnp.einsum("tf,df->td", grad_up_rows, back_up, preferred_element_type=f32)
    norm_grad2 = lax.psum(norm_part2, "mp")
    unused_two, pull_norm2 = jax.vjp(rms_norm, resid1, back_gmlp.astype(f32))
    resid_part1, grad_gmlp = pull_norm2(norm_grad2)
    resid1_grad = cot_rows + resid_part1
    out_grad = resid1_grad.astype(bf16)
    grad_out = jnp.einsum("th,td->hd", attended, out_grad, preferred_element_type=f32)
    attended_grad = (
        jnp.einsum("td,hd->th", out_grad, back_out, preferred_element_type=f32)
        .astype(bf16)
        .reshape(head_shape)
    )
    scores = score_block()
    probs_full = jnp.exp(scores - log_total)
    value_grad = jnp.einsum(
        "shqk,sqhe->skhe", probs_full.astype(bf16), attended_grad, preferred_element_type=f32
    )
    prob_grad = jnp.einsum(
        "sqhe,skhe->shqk", attended_grad, value_heads, preferred_element_type=f32
    )
    score_grad = (
        probs_full * (prob_grad - jnp.sum(prob_grad * probs_full, -1, keepdims=True))
    ).astype(bf16)
    query_grad = (
        jnp.einsum("shqk,skhe->sqhe", score_grad, key_rows, preferred_element_type=f32) * scale
    )
    key_grad = (
        jnp.einsum("shqk,sqhe->skhe", score_grad, queries, preferred_element_type=f32) * scale
    )
    width_local = local_heads * HD
    qkv_rows = jnp.stack(
        [
            rotate(query_grad, -places).reshape(-1, width_local),
            rotate(key_grad, -places).reshape(-1, width_local),
            value_grad.reshape(-1, width_local),
        ],
        1,
    ).astype(bf16)
    grad_qkv = jnp.einsum("td,tch->dch", normed, qkv_rows, preferred_element_type=f32)
    norm_part1 = jnp.einsum("tch,dch->td", qkv_rows, back_qkv, preferred_element_type=f32)
    norm_grad1 = lax.psum(norm_part1, "mp")
    unused_three, pull_norm1 = jax.vjp(rms_norm, resid0, back_gattn.astype(f32))
    resid_part0, grad_gattn = pull_norm1(norm_grad1)
    resid0_grad = (resid1_grad + resid_part0).astype(bf16)
    grad_in2 = jnp.einsum("th,td->hd", hidden, resid0_grad, preferred_element_type=f32)
    grad_b2 = jnp.sum(resid0_grad.astype(f32), 0)
    grad_res = jnp.einsum("tp,td->pd", inputs, resid0_grad, preferred_element_type=f32)
    hidden_grad = jnp.einsum("td,hd->th", resid0_grad, back_in2, preferred_element_type=f32)
    unused_four, pull_silu = jax.vjp(jax.nn.silu, pre_act)
    pre_grad = pull_silu(hidden_grad)[0].astype(bf16)
    grad_in1 = jnp.einsum("tp,th->ph", inputs, pre_grad, preferred_element_type=f32)
    grad_b1 = jnp.sum(pre_grad.astype(f32), 0)
    input_grad = jnp.einsum(
        "th,ph->tp", pre_grad, back_in1, preferred_element_type=f32
    ) + jnp.einsum("td,pd->tp", resid0_grad, back_res, preferred_element_type=f32)
    values_grad = input_grad[:, :patch_len] * keep_mask
    shares = tuple(
        (
            lax.psum_scatter(grad_in1, "fsdp", scatter_dimension=1, tiled=True),
            lax.psum_scatter(grad_b1, "fsdp", scatter_dimension=0, tiled=True),
            lax.psum_scatter(grad_in2, "fsdp", scatter_dimension=0, tiled=True),
            lax.psum_scatter(grad_b2, "fsdp", scatter_dimension=0, tiled=True),
            lax.psum_scatter(grad_res, "fsdp", scatter_dimension=1, tiled=True),
            lax.psum_scatter(grad_gattn, "fsdp", scatter_dimension=0, tiled=True),
            lax.psum_scatter(grad_qkv, "fsdp", scatter_dimension=0, tiled=True),
            lax.psum_scatter(grad_out, "fsdp", scatter_dimension=1, tiled=True),
            lax.psum_scatter(grad_gmlp, "fsdp", scatter_dimension=0, tiled=True),
            lax.psum_scatter(grad_up, "fsdp", scatter_dimension=0, tiled=True),
            lax.psum_scatter(grad_down, "fsdp", scatter_dimension=1, tiled=True),
        )
    )
    return (result, values_grad) + shares


def solution(mesh):
    in_specs = (
        P("fsdp", None),
        P("fsdp"),
        P(None, "fsdp"),
        P("fsdp"),
        P("fsdp", None),
        P("fsdp"),
        P(None, "fsdp"),
        P("fsdp"),
        P("fsdp", None, "mp"),
        P("mp", "fsdp"),
        P("fsdp"),
        P("fsdp", "mp"),
        P("mp", "fsdp"),
        P("fsdp", None),
    )
    out_specs = (
        P("fsdp", None),
        P("fsdp", None),
        P(None, "fsdp"),
        P("fsdp"),
        P("fsdp", None),
        P("fsdp"),
        P(None, "fsdp"),
        P("fsdp"),
        P("fsdp", None, "mp"),
        P("mp", "fsdp"),
        P("fsdp"),
        P("fsdp", "mp"),
        P("mp", "fsdp"),
    )
    return jax.shard_map(
        on_device, mesh=mesh, in_specs=in_specs, out_specs=out_specs, check_vma=False
    )
```

profile of v0, /device:TPU:10, one launch (start us, length us, event | category | flops | bytes accessed | tf_op | source)
XLA Modules:
  0.0 1254.7 jit_solution(667919393535561383)
XLA Ops:
  15.8 66.1 %all-reduce.9 = (bf16[1280]{0:T(1024)(128)(2,1)S(1)}, bf16[1280]{0:T(1024)(128)(2,1)S(1)}, bf16[1280]{0:T(1024)(128)(2,1)S(1)}, bf16[1280]{0:T(1024)(128)(2,1)}) all-reduce(bf16[1280]{0:T(1024)(128)(2,1)S(1)} %dynamic-update-slice.1, bf16[1280]{0:T(1024)(128)(2,1)S(1)} %dynamic-update-slice, ...), channel_id=1, replica_groups=mesh['fsdp'=16,'mp'=2] {'fsdp'}, use_global_device_ids=true, to_apply=%add.1 | all-reduce | flops 5120 | bytes 20480
  82.7 44.8 %all-gather = bf16[16,80,64]{1,2,0:T(8,128)(2,1)S(1)} all-gather(bf16[1,80,64]{1,2,0:T(8,128)(2,1)} %bitcast.81), channel_id=1, replica_groups=mesh['fsdp'=16,'mp'=2] {'fsdp'}, dimensions={0}, use_global_device_ids=true | all-gather | bytes 174080 | tf_op jit(solution)/shard_map/all_gather | solution.py:57
  127.9 38.5 %all-gather.1 = bf16[16,80,64]{1,2,0:T(8,128)(2,1)S(1)} all-gather(bf16[1,80,64]{1,2,0:T(8,128)(2,1)S(1)} %bitcast.82), channel_id=1, replica_groups=mesh['fsdp'=16,'mp'=2] {'fsdp'}, dimensions={0}, use_global_device_ids=true | all-gather | bytes 174080 | tf_op jit(solution)/shard_map/all_gather | solution.py:61
  175.0 4.0 fusion.35
  190.7 38.6 %all-gather.12.cloned.1.call-done = bf16[640,1280]{0,1:T(8,128)(2,1)} async-done(((bf16[640,80]{0,1:T(8,128)(2,1)}), bf16[640,1280]{0,1:T(8,128)(2,1)}) %all-gather.12.cloned.1.call-update) | async-done | bytes 1638416 | tf_op jit(solution)/shard_map/all_gather | solution.py:64
  234.0 18.6 %all-reduce.15.cloned.1.call-done = f32[256,1280]{1,0:T(8,128)} async-done(((f32[256,1280]{1,0:T(8,128)}), f32[256,1280]{1,0:T(8,128)}) %all-reduce.15.cloned.1.call-update) | async-done | bytes 1310736 | tf_op jit(solution)/shard_map/psum | solution.py:128
  254.1 59.7 %all-gather.14.cloned.1.call-done = bf16[1280,640]{1,0:T(8,128)(2,1)} async-done(((bf16[80,640]{1,0:T(8,128)(2,1)}), bf16[1280,640]{1,0:T(8,128)(2,1)}) %all-gather.14.cloned.1.call-update) | async-done | bytes 1638416 | tf_op jit(solution)/shard_map/all_gather | solution.py:66
  316.8 56.9 %all-gather.16.cloned.1.call-done = bf16[640,1280]{0,1:T(8,128)(2,1)} async-done(((bf16[640,80]{0,1:T(8,128)(2,1)}), bf16[640,1280]{0,1:T(8,128)(2,1)}) %all-gather.16.cloned.1.call-update) | async-done | bytes 1638416 | tf_op jit(solution)/shard_map/all_gather | solution.py:67
  373.7 4.7 add_convert_fusion.5
  384.8 16.1 %all-reduce.19.cloned.1.call-done = f32[256,1280]{1,0:T(8,128)} async-done(((f32[256,1280]{1,0:T(8,128)}), f32[256,1280]{1,0:T(8,128)}) %all-reduce.19.cloned.1.call-update) | async-done | bytes 1310736 | tf_op jit(solution)/shard_map/psum | solution.py:171
  402.5 21.4 %all-reduce.17.cloned.1.call-done = bf16[256,1280]{1,0:T(8,128)(2,1)} async-done(((bf16[256,1280]{1,0:T(8,128)(2,1)}), bf16[256,1280]{1,0:T(8,128)(2,1)}) %all-reduce.17.cloned.1.call-update) | async-done | bytes 655376 | tf_op jit(solution)/shard_map/psum | solution.py:134
  437.7 3.9 subtract_convert_fusion
  451.1 5.0 convolution_bitcast_fusion
  456.2 21.3 %all-reduce.21.cloned.1.call-done = f32[256,1280]{1,0:T(8,128)} async-done(((f32[256,1280]{1,0:T(8,128)}), f32[256,1280]{1,0:T(8,128)}) %all-reduce.21.cloned.1.call-update) | async-done | bytes 1310736 | tf_op jit(solution)/shard_map/psum | solution.py:210
  486.6 3.4 fusion.48
  499.8 4.0 fusion.50
  505.0 5.4 fusion.33
  511.2 65.2 %all-reduce.8 = (f32[1280]{0:T(1024)S(1)}, f32[1280]{0:T(1024)S(1)}, f32[1280]{0:T(1024)S(1)}, f32[1280]{0:T(1024)S(1)}) all-reduce(f32[1280]{0:T(1024)S(1)} %get-tuple-element.27, f32[1280]{0:T(1024)S(1)} %get-tuple-element.25, f32[1280]{0:T(1024)S(1)} %get-tuple-element.15, ...), channel_id=3, replica_groups=mesh['fsdp'=16,'mp'=2] {'fsdp'}, use_global_device_ids=true, to_apply=%region_13.14.clone | all-reduce | flops 5120 | bytes 40960
  581.5 46.6 %reduce-scatter.24.cloned.1.call-done = f32[80,64]{1,0:T(8,128)} async-done(((f32[1280,64]{1,0:T(8,128)}), f32[80,64]{1,0:T(8,128)}) %reduce-scatter.24.cloned.1.call-update) | async-done | bytes 20496
  629.6 86.2 %reduce-scatter.18.cloned.1.call-done = f32[80,640]{1,0:T(8,128)} async-done(((f32[1280,640]{1,0:T(8,128)}), f32[80,640]{1,0:T(8,128)}) %reduce-scatter.18.cloned.1.call-update) | async-done | bytes 204816 | tf_op jit(solution)/shard_map/reduce_scatter | solution.py:237
  715.9 85.1 %reduce-scatter.20.cloned.1.call-done = f32[640,80]{0,1:T(8,128)} async-done(((f32[640,1280]{0,1:T(8,128)}), f32[640,80]{0,1:T(8,128)}) %reduce-scatter.20.cloned.1.call-update) | async-done | bytes 204816 | tf_op jit(solution)/shard_map/reduce_scatter | solution.py:238
  800.9 84.7 %reduce-scatter.16.cloned.1.call-done = f32[640,80]{0,1:T(8,128)} async-done(((f32[640,1280]{0,1:T(8,128)}), f32[640,80]{0,1:T(8,128)}) %reduce-scatter.16.cloned.1.call-update) | async-done | bytes 204816 | tf_op jit(solution)/shard_map/reduce_scatter | solution.py:235
  885.6 150.4 %reduce-scatter.12.cloned.1.call-done = f32[80,1280]{1,0:T(8,128)} async-done(((f32[1280,1280]{1,0:T(8,128)}), f32[80,1280]{1,0:T(8,128)}) %reduce-scatter.12.cloned.1.call-update) | async-done | bytes 409616 | tf_op jit(solution)/shard_map/reduce_scatter | solution.py:230
  1036.0 212.2 %reduce-scatter.14.cloned.1.call-done = f32[80,3,640]{2,0,1:T(8,128)} async-done(((f32[1280,3,640]{2,0,1:T(8,128)}), f32[80,3,640]{2,0,1:T(8,128)}) %reduce-scatter.14.cloned.1.call-update) | async-done | bytes 614416 | tf_op jit(solution)/shard_map/reduce_scatter | solution.py:234
  (226 shorter events, 96.0 us)
Async XLA Ops:
  7.2 120.7 %copy-start.41 = (bf16[64,80]{1,0:T(8,128)(2,1)S(1)}, bf16[64,80]{1,0:T(8,128)(2,1)}, u32[]{:S(2)}) copy-start(bf16[64,80]{1,0:T(8,128)(2,1)} %param.20) | copy-start | bytes 30724
  7.2 162.6 %all-gather.8.cloned.1.call-start = ((), (), s32[]{:S(2)}) async-start(), calls=%async_computation.7 | async-start | bytes 3481600 | tf_op jit(solution)/shard_map/all_gather | solution.py:59
  7.9 166.5 %all-gather.10.cloned.1.call-start = ((), (), s32[]{:S(2)}) async-start(), calls=%async_computation.8 | async-start | bytes 5222400 | tf_op jit(solution)/shard_map/all_gather | solution.py:63
  8.7 220.7 %all-gather.12.cloned.1.call-start = ((), (), s32[]{:S(2)}) async-start(), calls=%async_computation.9 | async-start | bytes 1740800 | tf_op jit(solution)/shard_map/all_gather | solution.py:64
  9.4 243.2 %all-reduce.15.cloned.1.call-start = ((), (), s32[]{:S(2)}) async-start(), calls=%async_computation.10 | async-start | bytes 2621440 | tf_op jit(solution)/shard_map/psum | solution.py:128
  10.5 156.0 %copy-start.46 = (f32[256]{0:T(256)}, f32[256]{0:T(256)S(1)}, u32[]{:S(2)}) copy-start(f32[256]{0:T(256)S(1)} %sub.90) | copy-start | bytes 3076
  81.9 92.5 %copy-start.38 = (f32[1280]{0:T(1024)}, f32[1280]{0:T(1024)S(1)}, u32[]{:S(2)}) copy-start(f32[1280]{0:T(1024)S(1)} %convert_element_type.115) | copy-start | bytes 15364
  190.7 41.8 %copy-start.18 = (bf16[256,640]{1,0:T(8,128)(2,1)}, bf16[256,640]{1,0:T(8,128)(2,1)S(1)}, u32[]{:S(2)}) copy-start(bf16[256,640]{1,0:T(8,128)(2,1)S(1)} %convert_element_type.122) | copy-start | bytes 983044
  232.6 81.2 %all-gather.14.cloned.1.call-start = ((), (), s32[]{:S(2)}) async-start(), calls=%async_computation.11 | async-start | bytes 1740800 | tf_op jit(solution)/shard_map/all_gather | solution.py:66
  233.2 140.5 %all-gather.16.cloned.1.call-start = ((), (), s32[]{:S(2)}) async-start(), calls=%async_computation.12 | async-start | bytes 1740800 | tf_op jit(solution)/shard_map/all_gather | solution.py:67
  233.7 167.2 %all-reduce.19.cloned.1.call-start = ((), (), s32[]{:S(2)}) async-start(), calls=%async_computation.14 | async-start | bytes 2621440 | tf_op jit(solution)/shard_map/psum | solution.py:171
  380.9 43.1 %all-reduce.17.cloned.1.call-start = ((), (), s32[]{:S(2)}) async-start(), calls=%async_computation.13 | async-start | bytes 1310720 | tf_op jit(solution)/shard_map/psum | solution.py:134
  384.7 92.7 %all-reduce.21.cloned.1.call-start = ((), (), s32[]{:S(2)}) async-start(), calls=%async_computation.15 | async-start | bytes 2621440 | tf_op jit(solution)/shard_map/psum | solution.py:210
  456.2 123.9 %reduce-scatter.22.cloned.1.call-start = ((), (), s32[]{:S(2)}) async-start(), calls=%async_computation.21 | async-start | bytes 696320
  485.3 142.9 %reduce-scatter.24.cloned.1.call-start = ((), (), s32[]{:S(2)}) async-start(), calls=%async_computation.22 | async-start | bytes 696320
  486.6 229.3 %reduce-scatter.18.cloned.1.call-start = ((), (), s32[]{:S(2)}) async-start(), calls=%async_computation.19 | async-start | bytes 3481600 | tf_op jit(solution)/shard_map/reduce_scatter | solution.py:237
  490.1 310.8 %reduce-scatter.20.cloned.1.call-start = ((), (), s32[]{:S(2)}) async-start(), calls=%async_computation.20 | async-start | bytes 3481600 | tf_op jit(solution)/shard_map/reduce_scatter | solution.py:238
  493.7 391.9 %reduce-scatter.16.cloned.1.call-start = ((), (), s32[]{:S(2)}) async-start(), calls=%async_computation.18 | async-start | bytes 3481600 | tf_op jit(solution)/shard_map/reduce_scatter | solution.py:235
  498.5 537.5 %reduce-scatter.12.cloned.1.call-start = ((), (), s32[]{:S(2)}) async-start(), calls=%async_computation.16 | async-start | bytes 6963200 | tf_op jit(solution)/shard_map/reduce_scatter | solution.py:230
  503.8 744.4 %reduce-scatter.14.cloned.1.call-start = ((), (), s32[]{:S(2)}) async-start(), calls=%async_computation.17 | async-start | bytes 10444800 | tf_op jit(solution)/shard_map/reduce_scatter | solution.py:234
  510.4 68.3 %copy-start.30 = (bf16[1280,64]{0,1:T(8,128)(2,1)S(1)}, bf16[1280,64]{0,1:T(8,128)(2,1)}, u32[]{:S(2)}) copy-start(bf16[1280,64]{0,1:T(8,128)(2,1)} %copy-done.29) | copy-start | bytes 491524
  510.4 68.7 %copy-start.24 = (bf16[256,1280]{1,0:T(8,128)(2,1)S(1)}, bf16[256,1280]{1,0:T(8,128)(2,1)}, u32[]{:S(2)}) copy-start(bf16[256,1280]{1,0:T(8,128)(2,1)} %copy-done.23) | copy-start | bytes 1966084
  510.4 68.7 %copy-start.32 = (bf16[1280,64]{0,1:T(8,128)(2,1)S(1)}, bf16[1280,64]{0,1:T(8,128)(2,1)}, u32[]{:S(2)}) copy-start(bf16[1280,64]{0,1:T(8,128)(2,1)} %copy-done.31) | copy-start | bytes 491524
  510.4 69.0 %copy-start.47 = (f32[256]{0:T(256)S(1)}, f32[256]{0:T(256)}, u32[]{:S(2)}) copy-start(f32[256]{0:T(256)} %copy-done.46) | copy-start | bytes 3076
  (42 other events, 172.7 us)
Sparse Core Ops, SparseCore 0:
  10.8 70.6 all-gather.7
  84.1 85.1 all-gather.9
  172.0 57.2 all-gather.11
  232.7 19.8 all-reduce.14
  255.5 58.2 all-gather.13
  316.7 56.9 all-gather.15
  381.0 19.8 all-reduce.18
  403.8 20.1 all-reduce.16
  456.3 21.1 all-reduce.20
  485.4 67.0 reduce-scatter.21
  554.8 73.3 reduce-scatter.23
  630.9 84.9 reduce-scatter.17
  718.7 82.1 reduce-scatter.19
  803.7 81.8 reduce-scatter.15
  888.3 147.6 reduce-scatter.11
  1038.9 209.2 reduce-scatter.13
where the time goes:
time: 1260 us; the launch traced here: 1250 us
  waiting for transfers between devices  901 us (72%)
  blocking collectives  215 us (17%)
  matrix products  57.3 us (5%)
  local copies, waits for them, and re-layouts  43.2 us (3%)
  other arithmetic  21.6 us (2%)
  between operations  15.9 us (1%)
    reduce_scatter x1, waiting for transfers between devices, on_device(): lax.psum_scatter(grad_qkv, 'fsdp', scatter_dimension=0, tiled=True)  212 us
    reduce_scatter x1, waiting for transfers between devices, on_device(): lax.psum_scatter(grad_in2, 'fsdp', scatter_dimension=0, tiled=True)  150 us
    unnamed x2, blocking collectives  131 us
    reduce_scatter x1, waiting for transfers between devices, on_device(): lax.psum_scatter(grad_up, 'fsdp', scatter_dimension=0, tiled=True)  86.2 us
    reduce_scatter x1, waiting for transfers between devices, on_device(): lax.psum_scatter(grad_down, 'fsdp', scatter_dimension=1, tiled=True)  85.1 us
    reduce_scatter x1, waiting for transfers between devices, on_device(): lax.psum_scatter(grad_out, 'fsdp', scatter_dimension=1, tiled=True)  84.7 us
    all_gather x1, waiting for transfers between devices, on_device(): lax.all_gather(w_up, 'fsdp', axis=0, tiled=True)  59.7 us
    all_gather x1, waiting for transfers between devices, on_device(): lax.all_gather(w_down, 'fsdp', axis=1, tiled=True)  56.9 us
  transfers between devices with their start and end apart: 16, of which 13 were waited for; matrix products, arithmetic and copies ran while one was open for 5% of the time, Pallas kernels for 0%

commit v1 on v0

--- a/solution.py
+++ b/solution.py
@@ -53,6 +53,38 @@
 ):
     f32 = jnp.float32
     bf16 = jnp.bfloat16
+
+    def launch_table_on(w_in, dimension_no):
+        answer = lax.axis_index("fsdp")
+        big = lax.axis_size("fsdp")
+        all_rows, w2, built = (big, answer, w_in.shape[dimension_no])
+        near = range(all_rows)
+        z1 = map(lambda jj: (jj, (jj + 1) % all_rows), near)
+        b_next = range(all_rows)
+        state_now = map(lambda jj: (jj, (jj - 1) % all_rows), b_next)
+        bank = list(z1)
+        fields = list(state_now)
+        block_next = jnp.zeros(
+            (*w_in.shape[:dimension_no], all_rows * built, *w_in.shape[dimension_no + 1 :]),
+            w_in.dtype,
+        )
+        block_next = lax.dynamic_update_slice_in_dim(
+            block_next, w_in, w2 * built, axis=dimension_no
+        )
+        high = all_rows // 2
+        o_now = part_next = w_in
+        for m in tuple(range(1, high + 1)):
+            o_now = lax.ppermute(o_now, "fsdp", bank)
+            block_next = lax.dynamic_update_slice_in_dim(
+                block_next, o_now, (w2 - m) % all_rows * built, axis=dimension_no
+            )
+            if m < all_rows - high:
+                part_next = lax.ppermute(part_next, "fsdp", fields)
+                block_next = lax.dynamic_update_slice_in_dim(
+                    block_next, part_next, (w2 + m) % all_rows * built, axis=dimension_no
+                )
+        return block_next
+
     gathered = (
         lax.all_gather(w_in1, "fsdp", axis=1, tiled=True),
         lax.all_gather(b_in1, "fsdp", axis=0, tiled=True),
@@ -61,7 +93,7 @@
         lax.all_gather(w_res, "fsdp", axis=1, tiled=True),
         lax.all_gather(g_attn, "fsdp", axis=0, tiled=True),
         lax.all_gather(w_qkv, "fsdp", axis=0, tiled=True),
-        lax.all_gather(w_out, "fsdp", axis=1, tiled=True),
+        launch_table_on(w_out, 1),
         lax.all_gather(g_mlp, "fsdp", axis=0, tiled=True),
         lax.all_gather(w_up, "fsdp", axis=0, tiled=True),
         lax.all_gather(w_down, "fsdp", axis=1, tiled=True),

time: 1260 us -> 1340 us (1.063)
  waiting for transfers between devices: 901 us -> 956 us
  starting transfers between devices: 1.05 us -> 17.1 us
    ppermute x0 -> x15, waiting for transfers between devices: none -> 21.1 us  [the longest x8 21.1 us: launch_table_on(): o_now = lax.ppermute(o_now, 'fsdp', bank)]
    all_gather x1, waiting for transfers between devices: 38.6 us -> 58 us  [on_device(): lax.all_gather(w_out, 'fsdp', axis=1, tiled=True)]
    psum x1, waiting for transfers between devices: 18.6 us -> 35.9 us  [on_device(): lax.psum(jnp.dot(attended, full_out, preferred_element_type=f32), 'mp')]
    ppermute x0 -> x15, starting transfers between devices: none -> 16 us  [the longest x7 14.2 us: launch_table_on(): part_next = lax.ppermute(part_next, 'fsdp', fields)]
  transfers between devices with their start and end apart: 16 -> 31, of which waited for: 13 -> 20; matrix products, arithmetic and copies ran while one was open for 5% -> 5% of each run, Pallas kernels for 0% -> 0%
where the time goes in v1:
time: 1340 us; the launch traced here: 1330 us
  waiting for transfers between devices  956 us (71%)
  blocking collectives  215 us (16%)
  matrix products  58.5 us (4%)
  local copies, waits for them, and re-layouts  53.1 us (4%)
  other arithmetic  18.2 us (1%)
  starting transfers between devices  17.1 us (1%)
  between operations  16.1 us (1%)
    reduce_scatter x1, waiting for transfers between devices, on_device(): lax.psum_scatter(grad_qkv, 'fsdp', scatter_dimension=0, tiled=True)  212 us
    reduce_scatter x1, waiting for transfers between devices, on_device(): lax.psum_scatter(grad_in2, 'fsdp', scatter_dimension=0, tiled=True)  151 us
    unnamed x2, blocking collectives  132 us
    reduce_scatter x1, waiting for transfers between devices, on_device(): lax.psum_scatter(grad_up, 'fsdp', scatter_dimension=0, tiled=True)  85.9 us
    reduce_scatter x1, waiting for transfers between devices, on_device(): lax.psum_scatter(grad_down, 'fsdp', scatter_dimension=1, tiled=True)  84.7 us
    reduce_scatter x1, waiting for transfers between devices, on_device(): lax.psum_scatter(grad_out, 'fsdp', scatter_dimension=1, tiled=True)  84.7 us
    all_gather x1, waiting for transfers between devices, on_device(): lax.all_gather(w_up, 'fsdp', axis=0, tiled=True)  59.7 us
    all_gather x1, waiting for transfers between devices, on_device(): lax.all_gather(w_out, 'fsdp', axis=1, tiled=True)  58 us
  transfers between devices with their start and end apart: 31, of which 20 were waited for; matrix products, arithmetic and copies ran while one was open for 5% of the time, Pallas kernels for 0%

profile of v1, /device:TPU:10, one launch (start us, length us, event | category | flops | bytes accessed | tf_op | source)
XLA Modules:
  0.0 1333.9 jit_solution(14566133085204311793)
XLA Ops:
  16.2 66.8 %all-reduce.9 = (bf16[1280]{0:T(1024)(128)(2,1)S(1)}, bf16[1280]{0:T(1024)(128)(2,1)S(1)}, bf16[1280]{0:T(1024)(128)(2,1)S(1)}, bf16[1280]{0:T(1024)(128)(2,1)}) all-reduce(bf16[1280]{0:T(1024)(128)(2,1)S(1)} %dynamic-update-slice.1, bf16[1280]{0:T(1024)(128)(2,1)S(1)} %dynamic-update-slice, ...), channel_id=1, replica_groups=mesh['fsdp'=16,'mp'=2] {'fsdp'}, use_global_device_ids=true, to_apply=%add.1 | all-reduce | flops 5120 | bytes 20480
  83.0 43.6 %all-gather = bf16[16,80,64]{1,2,0:T(8,128)(2,1)S(1)} all-gather(bf16[1,80,64]{1,2,0:T(8,128)(2,1)} %bitcast.81), channel_id=1, replica_groups=mesh['fsdp'=16,'mp'=2] {'fsdp'}, dimensions={0}, use_global_device_ids=true | all-gather | bytes 174080 | tf_op jit(solution)/shard_map/all_gather | solution.py:89
  127.3 39.6 %all-gather.1 = bf16[16,80,64]{1,2,0:T(8,128)(2,1)S(1)} all-gather(bf16[1,80,64]{1,2,0:T(8,128)(2,1)S(1)} %bitcast.82), channel_id=1, replica_groups=mesh['fsdp'=16,'mp'=2] {'fsdp'}, dimensions={0}, use_global_device_ids=true | all-gather | bytes 174080 | tf_op jit(solution)/shard_map/all_gather | solution.py:93
  182.8 3.9 collective-permute-done.4
  211.7 5.0 collective-permute-done.14
  221.0 4.0 fusion.35
  240.4 35.9 %all-reduce.15.cloned.1.call-done = f32[256,1280]{1,0:T(8,128)} async-done(((f32[256,1280]{1,0:T(8,128)}), f32[256,1280]{1,0:T(8,128)}) %all-reduce.15.cloned.1.call-update) | async-done | bytes 1310736 | tf_op jit(solution)/shard_map/psum | solution.py:160
  277.9 59.7 %all-gather.12.cloned.1.call-done = bf16[1280,640]{1,0:T(8,128)(2,1)} async-done(((bf16[80,640]{1,0:T(8,128)(2,1)}), bf16[1280,640]{1,0:T(8,128)(2,1)}) %all-gather.12.cloned.1.call-update) | async-done | bytes 1638416 | tf_op jit(solution)/shard_map/all_gather | solution.py:98
  340.5 56.9 %all-gather.14.cloned.1.call-done = bf16[640,1280]{0,1:T(8,128)(2,1)} async-done(((bf16[640,80]{0,1:T(8,128)(2,1)}), bf16[640,1280]{0,1:T(8,128)(2,1)}) %all-gather.14.cloned.1.call-update) | async-done | bytes 1638416 | tf_op jit(solution)/shard_map/all_gather | solution.py:99
  397.4 4.7 add_convert_fusion.5
  409.5 15.2 %all-reduce.19.cloned.1.call-done = f32[256,1280]{1,0:T(8,128)} async-done(((f32[256,1280]{1,0:T(8,128)}), f32[256,1280]{1,0:T(8,128)}) %all-reduce.19.cloned.1.call-update) | async-done | bytes 1310736 | tf_op jit(solution)/shard_map/psum | solution.py:203
  426.3 21.4 %all-reduce.17.cloned.1.call-done = bf16[256,1280]{1,0:T(8,128)(2,1)} async-done(((bf16[256,1280]{1,0:T(8,128)(2,1)}), bf16[256,1280]{1,0:T(8,128)(2,1)}) %all-reduce.17.cloned.1.call-update) | async-done | bytes 655376 | tf_op jit(solution)/shard_map/psum | solution.py:166
  451.1 58.0 %all-gather.16.cloned.1.call-done = bf16[640,1280]{0,1:T(8,128)(2,1)} async-done(((bf16[640,80]{0,1:T(8,128)(2,1)}), bf16[640,1280]{0,1:T(8,128)(2,1)}) %all-gather.16.cloned.1.call-update) | async-done | bytes 1638416 | tf_op jit(solution)/shard_map/all_gather | solution.py:178
  531.8 5.3 convolution_bitcast_fusion
  537.2 19.9 %all-reduce.21.cloned.1.call-done = f32[256,1280]{1,0:T(8,128)} async-done(((f32[256,1280]{1,0:T(8,128)}), f32[256,1280]{1,0:T(8,128)}) %all-reduce.21.cloned.1.call-update) | async-done | bytes 1310736 | tf_op jit(solution)/shard_map/psum | solution.py:242
  579.8 4.0 fusion.50
  585.0 5.5 fusion.33
  591.2 65.3 %all-reduce.8 = (f32[1280]{0:T(1024)S(1)}, f32[1280]{0:T(1024)S(1)}, f32[1280]{0:T(1024)S(1)}, f32[1280]{0:T(1024)S(1)}) all-reduce(f32[1280]{0:T(1024)S(1)} %get-tuple-element.27, f32[1280]{0:T(1024)S(1)} %get-tuple-element.25, f32[1280]{0:T(1024)S(1)} %get-tuple-element.15, ...), channel_id=3, replica_groups=mesh['fsdp'=16,'mp'=2] {'fsdp'}, use_global_device_ids=true, to_apply=%region_13.14.clone | all-reduce | flops 5120 | bytes 40960
  661.6 46.1 %reduce-scatter.24.cloned.1.call-done = f32[80,64]{1,0:T(8,128)} async-done(((f32[1280,64]{1,0:T(8,128)}), f32[80,64]{1,0:T(8,128)}) %reduce-scatter.24.cloned.1.call-update) | async-done | bytes 20496
  709.2 85.9 %reduce-scatter.18.cloned.1.call-done = f32[80,640]{1,0:T(8,128)} async-done(((f32[1280,640]{1,0:T(8,128)}), f32[80,640]{1,0:T(8,128)}) %reduce-scatter.18.cloned.1.call-update) | async-done | bytes 204816 | tf_op jit(solution)/shard_map/reduce_scatter | solution.py:269
  795.1 84.7 %reduce-scatter.20.cloned.1.call-done = f32[640,80]{0,1:T(8,128)} async-done(((f32[640,1280]{0,1:T(8,128)}), f32[640,80]{0,1:T(8,128)}) %reduce-scatter.20.cloned.1.call-update) | async-done | bytes 204816 | tf_op jit(solution)/shard_map/reduce_scatter | solution.py:270
  879.8 84.7 %reduce-scatter.16.cloned.1.call-done = f32[640,80]{0,1:T(8,128)} async-done(((f32[640,1280]{0,1:T(8,128)}), f32[640,80]{0,1:T(8,128)}) %reduce-scatter.16.cloned.1.call-update) | async-done | bytes 204816 | tf_op jit(solution)/shard_map/reduce_scatter | solution.py:267
  964.5 150.6 %reduce-scatter.12.cloned.1.call-done = f32[80,1280]{1,0:T(8,128)} async-done(((f32[1280,1280]{1,0:T(8,128)}), f32[80,1280]{1,0:T(8,128)}) %reduce-scatter.12.cloned.1.call-update) | async-done | bytes 409616 | tf_op jit(solution)/shard_map/reduce_scatter | solution.py:262
  1115.2 212.2 %reduce-scatter.14.cloned.1.call-done = f32[80,3,640]{2,0,1:T(8,128)} async-done(((f32[1280,3,640]{2,0,1:T(8,128)}), f32[80,3,640]{2,0,1:T(8,128)}) %reduce-scatter.14.cloned.1.call-update) | async-done | bytes 614416 | tf_op jit(solution)/shard_map/reduce_scatter | solution.py:266
  (273 shorter events, 138.9 us)
Async XLA Ops:
  7.2 210.1 %all-gather.8.cloned.1.call-start = ((), (), s32[]{:S(2)}) async-start(), calls=%async_computation.7 | async-start | bytes 3481600 | tf_op jit(solution)/shard_map/all_gather | solution.py:91
  7.9 213.0 %all-gather.10.cloned.1.call-start = ((), (), s32[]{:S(2)}) async-start(), calls=%async_computation.8 | async-start | bytes 5222400 | tf_op jit(solution)/shard_map/all_gather | solution.py:95
  8.7 267.6 %all-reduce.15.cloned.1.call-start = ((), (), s32[]{:S(2)}) async-start(), calls=%async_computation.9 | async-start | bytes 2621440 | tf_op jit(solution)/shard_map/psum | solution.py:160
  8.7 163.9 %collective-permute-start = (bf16[640,80]{0,1:T(8,128)(2,1)}, bf16[640,80]{0,1:T(8,128)(2,1)S(1)}, u32[]{:S(2)}, u32[]{:S(2)}) collective-permute-start(bf16[640,80]{0,1:T(8,128)(2,1)} %param.23), channel_id=1, source_target_pairs={{0,2},{2,4},{4,6},{6,8},{8,10},{10,12},{12,14},{14,16},{16,18},{18... | collective-permute-start | bytes 307208 | tf_op jit(solution)/shard_map/ppermute | solution.py:77
  10.3 162.4 %collective-permute-start.1 = (bf16[640,80]{0,1:T(8,128)(2,1)}, bf16[640,80]{0,1:T(8,128)(2,1)S(1)}, u32[]{:S(2)}, u32[]{:S(2)}) collective-permute-start(bf16[640,80]{0,1:T(8,128)(2,1)} %param.23), channel_id=1, source_target_pairs={{0,30},{2,0},{4,2},{6,4},{8,6},{10,8},{12,10},{14,12},{16,14},{18,... | collective-permute-start | bytes 307208 | tf_op jit(solution)/shard_map/ppermute | solution.py:82
  172.6 6.8 collective-permute-start.2
  172.6 6.8 collective-permute-start.3
  179.5 7.3 collective-permute-start.4
  179.5 7.3 collective-permute-start.5
  198.4 6.5 collective-permute-start.10
  198.4 6.5 collective-permute-start.11
  239.2 98.3 %all-gather.12.cloned.1.call-start = ((), (), s32[]{:S(2)}) async-start(), calls=%async_computation.10 | async-start | bytes 1740800 | tf_op jit(solution)/shard_map/all_gather | solution.py:98
  239.8 157.7 %all-gather.14.cloned.1.call-start = ((), (), s32[]{:S(2)}) async-start(), calls=%async_computation.11 | async-start | bytes 1740800 | tf_op jit(solution)/shard_map/all_gather | solution.py:99
  240.3 184.3 %all-reduce.19.cloned.1.call-start = ((), (), s32[]{:S(2)}) async-start(), calls=%async_computation.13 | async-start | bytes 2621440 | tf_op jit(solution)/shard_map/psum | solution.py:203
  404.6 43.1 %all-reduce.17.cloned.1.call-start = ((), (), s32[]{:S(2)}) async-start(), calls=%async_computation.12 | async-start | bytes 1310720 | tf_op jit(solution)/shard_map/psum | solution.py:166
  408.7 100.4 %all-gather.16.cloned.1.call-start = ((), (), s32[]{:S(2)}) async-start(), calls=%async_computation.14 | async-start | bytes 1740800 | tf_op jit(solution)/shard_map/all_gather | solution.py:178
  409.4 147.7 %all-reduce.21.cloned.1.call-start = ((), (), s32[]{:S(2)}) async-start(), calls=%async_computation.15 | async-start | bytes 2621440 | tf_op jit(solution)/shard_map/psum | solution.py:242
  537.2 123.0 %reduce-scatter.22.cloned.1.call-start = ((), (), s32[]{:S(2)}) async-start(), calls=%async_computation.21 | async-start | bytes 696320
  565.0 142.8 %reduce-scatter.24.cloned.1.call-start = ((), (), s32[]{:S(2)}) async-start(), calls=%async_computation.22 | async-start | bytes 696320
  566.3 228.8 %reduce-scatter.18.cloned.1.call-start = ((), (), s32[]{:S(2)}) async-start(), calls=%async_computation.19 | async-start | bytes 3481600 | tf_op jit(solution)/shard_map/reduce_scatter | solution.py:269
  570.1 309.8 %reduce-scatter.20.cloned.1.call-start = ((), (), s32[]{:S(2)}) async-start(), calls=%async_computation.20 | async-start | bytes 3481600 | tf_op jit(solution)/shard_map/reduce_scatter | solution.py:270
  573.7 390.8 %reduce-scatter.16.cloned.1.call-start = ((), (), s32[]{:S(2)}) async-start(), calls=%async_computation.18 | async-start | bytes 3481600 | tf_op jit(solution)/shard_map/reduce_scatter | solution.py:267
  578.5 536.7 %reduce-scatter.12.cloned.1.call-start = ((), (), s32[]{:S(2)}) async-start(), calls=%async_computation.16 | async-start | bytes 6963200 | tf_op jit(solution)/shard_map/reduce_scatter | solution.py:262
  583.8 743.5 %reduce-scatter.14.cloned.1.call-start = ((), (), s32[]{:S(2)}) async-start(), calls=%async_computation.17 | async-start | bytes 10444800 | tf_op jit(solution)/shard_map/reduce_scatter | solution.py:266
  (57 other events, 1119.8 us)
Sparse Core Ops, SparseCore 0:
  10.8 70.6 all-gather.7
  84.1 88.4 all-gather.9
  239.3 36.9 all-reduce.14
  279.2 58.2 all-gather.11
  340.4 56.9 all-gather.13
  404.7 19.8 all-reduce.18
  427.5 20.1 all-reduce.16
  450.8 58.2 all-gather.15
  537.3 19.8 all-reduce.20
  565.1 66.9 reduce-scatter.21
  634.4 73.2 reduce-scatter.23
  710.4 84.6 reduce-scatter.17
  798.0 81.8 reduce-scatter.19
  882.6 81.8 reduce-scatter.15
  967.3 147.8 reduce-scatter.11
  1118.0 209.2 reduce-scatter.13
